TPU v7x, 128 devices: a whole 4x4x4 slice. The times are simulated.
128 devices in a mesh: ctx: 32 (over y, z, core), exp: 4 (over x).
Axes of the slice: x: 4, y: 4, z: 4, core: 2. Of those that a mesh axis runs over, the one named last changes fastest.
Arguments:
- inputs: bfloat16 [4096, 4096], P('ctx', 'exp'), may hold values from -6 to 6
- gate_input: bfloat16 [4096, 4096], P('ctx', 'exp')
- b_proj: bfloat16 [4096, 128], P('ctx'), may hold values from -0.5 to 0.5
- c_proj: bfloat16 [4096, 128], P('ctx'), may hold values from -6 to 6
- step_size: float32 [64, 4096], P('exp', 'ctx'), may hold values from 0.03 to 0.3
- decay_rate: float32 [64, 4096], P('exp', 'ctx'), as said below
- skip_gain: float32 [64], P('exp'), may hold values from 0.5 to 2
- start_state: float32 [64, 64, 128], P('exp'), may hold values from -3 to 3
- norm_gain: float32 [4096], P('exp'), may hold values from 0.5 to 1.5
- out_proj: bfloat16 [4096, 4096], P('exp', 'ctx'), may hold values from -0.09375 to 0.09375
- residual: bfloat16 [4096, 4096], P('ctx'), may hold values from -6 to 6
- moe_gain: float32 [4096], replicated, may hold values from 0.5 to 1.5
- w_gate: bfloat16 [32, 4096, 3584], P('ctx', None, 'exp'), may hold values from -0.09375 to 0.09375
- w_up: bfloat16 [32, 4096, 3584], P('ctx', None, 'exp'), may hold values from -0.09375 to 0.09375
- w_down: bfloat16 [32, 3584, 4096], P('ctx', 'exp'), may hold values from -0.0625 to 0.0625
- route_ids: int32 [4096, 2], P('ctx'), may hold values from 0 to 15, all different within a row; in each aligned block of 32 rows (0 to 31, 32 to 63, ...) at most 8 rows name the same one
- route_gates: float32 [4096, 2], P('ctx'), may hold values from 0.3 to 1
Outputs:
- output: bfloat16 [4096, 4096], P(('ctx', 'exp'))
Inputs may be any that keep to these rules, and one draw needn't show every extreme that they name: `route_ids`: each row names two different experts. In each aligned block of 32 rows no expert is named more than 8 times, a bound that some block reaches. `decay_rate`: Non-negative.
All inputs are finite; a program needn't handle non-finite values.
Results may differ from a plain program's by a relative error of at most 0.02.
Values may be sent and summed in bfloat16 or wider, within the bound.
A program may use at most 128 MiB of HBM per device.

v0:
```python
import jax
import jax.numpy as jnp
from jax import lax
from jax.sharding import PartitionSpec as P

PAIR = 2
eps_norm = 1e-05
top_precision = lax.Precision.HIGHEST


def entering(x, axis, join, neutral):
    place = lax.axis_index(axis)
    decay, state = x
    packed = jnp.concatenate(
        [state, jnp.broadcast_to(decay[:, None, None], (state.shape[0], 1, state.shape[2]))], axis=1
    )
    gathered = lax.all_gather(packed.astype(jnp.bfloat16), axis)
    start = jax.tree.map(lambda a, e: jnp.zeros_like(a) + jnp.asarray(e, a.dtype), x, neutral)

    def one(hop, carry):
        block = lax.dynamic_index_in_dim(gathered, hop, 0, False).astype(jnp.float32)
        return join(carry, (block[:, -1, 0], block[:, :-1, :]))

    return lax.fori_loop(0, place, one, start)


def later_state(earlier, later):
    first_decay, first_state = earlier
    second_decay, second_state = later
    return (first_decay * second_decay, second_decay[:, None, None] * first_state + second_state)


def route_ranks(quarter_ids, experts):
    flattened = quarter_ids.reshape(-1)
    onehot = (flattened[:, None] == jnp.arange(experts, dtype=jnp.int32)[None, :]).astype(jnp.int32)
    running = jnp.cumsum(onehot, axis=0)
    rank_ids = jnp.sum(onehot * running, axis=1) - 1
    return (flattened, rank_ids)


def place_rows(normed, quarter_ids, experts, capacity):
    flattened, rank_ids = route_ranks(quarter_ids, experts)
    slot_ids = rank_ids * experts + flattened
    matches = (
        jnp.arange(capacity * experts, dtype=jnp.int32)[:, None] == slot_ids[None, :]
    ).astype(jnp.bfloat16)
    doubled = jnp.repeat(normed, quarter_ids.shape[1], axis=0)
    placed = jnp.dot(matches, doubled, preferred_element_type=jnp.float32).astype(jnp.bfloat16)
    return placed.reshape(capacity, experts, normed.shape[1])


def rms_rows(values, gain_vec):
    scaling = lax.rsqrt(jnp.mean(values * values, axis=1, keepdims=True) + eps_norm)
    return (values * scaling * gain_vec[None, :]).astype(jnp.bfloat16)


def local(
    inputs,
    gate_input,
    b_proj,
    c_proj,
    step_size,
    decay_rate,
    skip_gain,
    start_state,
    norm_gain,
    out_proj,
    residual,
    moe_gain,
    w_gate,
    w_up,
    w_down,
    route_ids,
    route_gates,
):
    tok_ctx = inputs.shape[0]
    head_count = step_size.shape[0]
    head_dim = inputs.shape[1] // head_count
    model_width = residual.shape[1]
    n_ctx = lax.axis_size("ctx")
    n_exp = lax.axis_size("exp")
    experts = n_ctx // PAIR
    tok_quarter = tok_ctx // n_exp
    capacity = 4 * tok_quarter // experts
    x_local = inputs.astype(jnp.float32).reshape(tok_ctx, head_count, head_dim)
    b_local = b_proj.astype(jnp.float32)
    c_local = c_proj.astype(jnp.float32)
    cumulative = jnp.cumsum(decay_rate, axis=1)
    span_total = cumulative[:, -1]
    sequence_indices = jnp.arange(tok_ctx, dtype=jnp.int32)
    causal = sequence_indices[:, None] >= sequence_indices[None, :]
    spread = jnp.where(causal[None], cumulative[:, :, None] - cumulative[:, None, :], 0.0)
    scores = jnp.dot(c_local, b_local.T, precision=top_precision)
    mixing = jnp.where(causal[None], jnp.exp(-spread), 0.0) * scores[None] * step_size[:, None, :]
    inside_part = jnp.einsum("hts,shp->thp", mixing, x_local, precision=top_precision)
    ending = jnp.exp(-(span_total[:, None] - cumulative)) * step_size
    local_state = jnp.einsum("hs,shp,sn->hpn", ending, x_local, b_local, precision=top_precision)
    prior_decay, prior_state = entering(
        (jnp.exp(-span_total), local_state),
        "ctx",
        later_state,
        (jnp.ones_like(span_total), jnp.zeros_like(local_state)),
    )
    incoming = prior_state + prior_decay[:, None, None] * start_state
    carried = (
        jnp.einsum("hpn,tn->thp", incoming, c_local, precision=top_precision)
        * jnp.exp(-cumulative).T[:, :, None]
    )
    ssm_out = inside_part + carried + skip_gain[None, :, None] * x_local
    gated_out = ssm_out.reshape(tok_ctx, head_count * head_dim) * jax.nn.silu(
        gate_input.astype(jnp.float32)
    )
    squares = lax.psum(jnp.sum(gated_out * gated_out, axis=1), "exp")
    scaling = lax.rsqrt(squares / (head_count * head_dim * n_exp) + eps_norm)
    normed_mix = (gated_out * scaling[:, None] * norm_gain[None, :]).astype(jnp.bfloat16)
    partial_value = jnp.dot(
        normed_mix,
        lax.all_gather(out_proj, "ctx", axis=1, tiled=True),
        preferred_element_type=jnp.float32,
    )
    gate_rows = w_gate[0]
    up_rows = w_up[0]
    down_rows = w_down[0]
    piece_width = gate_rows.shape[1]
    first_row = lax.axis_index("exp") * tok_quarter
    own_ids = lax.dynamic_slice_in_dim(route_ids, first_row, tok_quarter, 0)
    own_gates = lax.dynamic_slice_in_dim(route_gates, first_row, tok_quarter, 0)
    mixed_all = lax.psum(partial_value.astype(jnp.bfloat16), "exp").astype(jnp.float32)
    hidden_all = residual.astype(jnp.float32) + mixed_all
    moe_all = rms_rows(hidden_all, moe_gain)

    def place_quarter(quarter_rows, quarter_ids):
        return place_rows(quarter_rows, quarter_ids, experts, capacity)

    placed = jax.vmap(place_quarter)(
        moe_all.reshape(n_exp, tok_quarter, model_width),
        route_ids.reshape(n_exp, tok_quarter, route_ids.shape[1]),
    )
    placed = placed.reshape(n_exp * capacity, experts, model_width)
    outgoing = jnp.repeat(placed, PAIR, axis=1)
    arrived = lax.all_to_all(outgoing, "ctx", split_axis=1, concat_axis=1, tiled=True)
    flattened = arrived.reshape(-1, model_width)
    gate_val = jnp.dot(flattened, gate_rows, preferred_element_type=jnp.float32)
    up_val = jnp.dot(flattened, up_rows, preferred_element_type=jnp.float32)
    activated = (jax.nn.silu(gate_val) * up_val).astype(jnp.bfloat16)
    hidden = activated.reshape(arrived.shape[0], arrived.shape[1], piece_width)
    hidden_own = lax.dynamic_slice_in_dim(hidden_all, first_row, tok_quarter, 0)
    product = jnp.dot(
        hidden.reshape(-1, piece_width), down_rows, preferred_element_type=jnp.float32
    )
    rounded = lax.optimization_barrier(product.astype(jnp.bfloat16)).astype(jnp.float32)
    summed = lax.psum_scatter(
        rounded.reshape(lax.axis_size("exp") * capacity, hidden.shape[1], model_width).astype(
            jnp.bfloat16
        ),
        "exp",
        scatter_dimension=0,
        tiled=True,
    )
    halves = lax.all_to_all(summed, "ctx", split_axis=1, concat_axis=1, tiled=True)
    flattened, rank_ids = route_ranks(own_ids, experts)
    base_rows = rank_ids * n_ctx + flattened * PAIR
    fetch_rows = base_rows[:, None] + jnp.arange(PAIR, dtype=jnp.int32)[None, :]
    fetched = halves.reshape(capacity * n_ctx, model_width)[fetch_rows]
    expert_out = jnp.sum(fetched.astype(jnp.float32), axis=1)
    weighted = expert_out * own_gates.reshape(-1)[:, None]
    moe_out = jnp.sum(weighted.reshape(tok_quarter, -1, model_width), axis=1)
    return (hidden_own + moe_out).astype(jnp.bfloat16)


def solution(mesh):
    in_specs = (
        P("ctx", "exp"),
        P("ctx", "exp"),
        P("ctx", None),
        P("ctx", None),
        P("exp", "ctx"),
        P("exp", "ctx"),
        P("exp"),
        P("exp", None, None),
        P("exp"),
        P("exp", "ctx"),
        P("ctx", None),
        P(),
        P("ctx", None, "exp"),
        P("ctx", None, "exp"),
        P("ctx", "exp", None),
        P("ctx", None),
        P("ctx", None),
    )
    out_specs = P(("ctx", "exp"), None)
    return jax.shard_map(local, mesh=mesh, in_specs=in_specs, out_specs=out_specs, check_vma=False)
```

profile of v0, /device:TPU:1, one launch (start us, length us, event | category | flops | bytes accessed | tf_op | source)
XLA Modules:
  0.0 688.3 jit_solution(15999288479080339872)
XLA Ops:
  6.5 1.0 reduce_window_sum.33
  7.7 0.8 exponential_bitcast_fusion
  8.5 1.1 copy.109
  9.6 0.4 fusion.11
  10.2 0.7 copy.110
  11.0 0.7 all-gather.5.cloned.1.call-update
  11.8 0.9 fusion.42
  12.6 55.4 %all-gather.3.cloned.1.call-done = bf16[32,16,65,128]{3,1,2,0:T(8,128)(2,1)} async-done(((bf16[1,16,65,128]{3,1,2,0:T(8,128)(2,1)}), bf16[32,16,65,128]{3,1,2,0:T(8,128)(2,1)}) %all-gather.3.cloned.1.call-update) | async-done | bytes 8519696 | tf_op jit(solution)/shard_map/all_gather | solution.py:17
  68.1 2.4 broadcast_in_dim.28
  70.5 7.9 %while.12 = (s32[]{:T(128)}, f32[16]{0:T(128)S(1)}, f32[16,64,128]{0,2,1:T(8,128)}, s32[]{:T(128)}, bf16[32,16,65,128]{3,1,2,0:T(8,128)(2,1)}, /*index=5*/s32[]{:T(128)}, s32[]{:T(128)}, s32[]{:T(128)}) while((s32[]{:T(128)}, f32[16]{0:T(128)S(1)}, f32[16,64,128]{0,2,1:T(8,128)}, s32[]{:T(128)}, bf16[32,16,65,128]{3,1,2,0:T(8,128)(2,1)}, ...), condition=%wide.region_2.3_spmd, body=%wide.region_1.2_spmd.sunk | while | flops 395285 | bytes 3437051 | solution.py:24
  70.5 1.0 constant_dynamic-slice_fusion.4
  71.5 1.4 copy.132
  72.9 0.5 bitcast_convert_fusion.2
  73.4 5.0 slice_add_fusion.2
  78.5 3.1 copy.112
  81.6 0.5 fusion.10
  82.1 1.4 fusion.9
  83.5 0.2 copy.115
  83.7 0.2 multiply_reduce_fusion.2
  83.9 8.4 %psum.14 = f32[128]{0:T(128)S(1)} all-reduce(f32[128]{0:T(128)S(1)} %multiply_reduce_fusion.2), channel_id=1, replica_groups=mesh['ctx'=32,'exp'=4] {'exp'}, use_global_device_ids=true, to_apply=%region_4.5 | all-reduce | flops 128 | bytes 1024 | tf_op jit(solution)/shard_map/psum | solution.py:113
  92.3 37.1 %all-gather.5.cloned.1.call-done = bf16[1024,4096]{1,0:T(8,128)(2,1)} async-done(((bf16[1024,128]{1,0:T(8,128)(2,1)}), bf16[1024,4096]{1,0:T(8,128)(2,1)}) %all-gather.5.cloned.1.call-update) | async-done | bytes 8388624 | tf_op jit(solution)/shard_map/all_gather | solution.py:118
  129.5 5.8 convolution_convert_fusion.2
  135.3 0.3 reduce-scatter.4.cloned.1.call-start
  136.1 0.2 select_reduce_fusion
  136.3 240.4 %all-reduce.2.cloned.1.call-done = bf16[128,4096]{1,0:T(8,128)(2,1)} async-done(((bf16[128,4096]{1,0:T(8,128)(2,1)}), bf16[128,4096]{1,0:T(8,128)(2,1)}) %all-reduce.2.cloned.1.call-update) | async-done | bytes 1048592 | tf_op jit(solution)/shard_map/psum | solution.py:128
  376.8 3.0 convert_add_fusion
  379.8 0.4 multiply_convert_fusion.1
  380.2 3.4 broadcast_in_dim.30
  383.6 2.7 reshape.163
  386.4 1.4 convolution_convert_fusion.1
  387.8 2.3 copy.117
  390.1 4.3 broadcast_in_dim.31
  394.3 105.3 %all_to_all.10 = bf16[32,32,4096]{2,0,1:T(8,128)(2,1)} all-to-all(bf16[32,32,4096]{2,0,1:T(8,128)(2,1)} %bitcast.70), channel_id=1, replica_groups=mesh['ctx'=32,'exp'=4] {'ctx'}, dimensions={1} | all-to-all | bytes 16777216 | tf_op jit(solution)/shard_map/all_to_all | solution.py:141
  499.6 11.3 %copy.118 = bf16[32,32,4096]{2,1,0:T(8,128)(2,1)} copy(bf16[32,32,4096]{2,0,1:T(8,128)(2,1)} %all_to_all.10) | data formatting | bytes 16777216 | tf_op jit(solution)/shard_map/all_to_all | solution.py:141
  511.0 12.7 %fusion.2 = f32[1024,896]{1,0:T(8,128)S(1)} fusion(bf16[1024,4096]{1,0:T(8,128)(2,1)} %bitcast.72, bf16[1,4096,896]{2,1,0:T(8,128)(2,1)} %param.32), kind=kOutput, calls=%fused_computation.8 | convolution fusion | flops 7516192768 | bytes 19398656 | tf_op jit(solution)/shard_map/dot_general | solution.py:144
  523.7 9.2 %multiply_convert_fusion = bf16[1024,896]{1,0:T(8,128)(2,1)S(1)} fusion(f32[1024,896]{1,0:T(8,128)S(1)} %fusion.2, bf16[1024,4096]{1,0:T(8,128)(2,1)S(1)} %bitcast.73, bf16[1,4096,896]{2,1,0:T(8,128)(2,1)S(1)} %bitcast.81), kind=kOutput, calls=%fused_computation.14 | convolution fusion | flops 7521697792 | bytes 21233664 | tf_op jit(solution)/shard_map/dot_general | solution.py:143
  532.9 11.3 %convolution_convert_fusion = bf16[1024,4096]{1,0:T(8,128)(2,1)} fusion(bf16[1024,896]{1,0:T(8,128)(2,1)S(1)} %multiply_convert_fusion, bf16[1,896,4096]{2,1,0:T(8,128)(2,1)S(1)} %bitcast.83), kind=kOutput, calls=%fused_computation.6 | convolution fusion | flops 7520387072 | bytes 17563648 | tf_op jit(solution)/shard_map/dot_general | solution.py:148
  544.1 11.3 %copy.130 = bf16[4,8,32,4096]{3,1,2,0:T(8,128)(2,1)} copy(bf16[4,8,32,4096]{3,2,1,0:T(8,128)(2,1)} %bitcast.74) | data formatting | bytes 16777216
  555.5 77.8 %reduce-scatter.4.cloned.1.call-done = bf16[8,131072]{1,0:T(8,128)(2,1)} async-done(((bf16[32,131072]{1,0:T(8,128)(2,1)}), bf16[8,131072]{1,0:T(8,128)(2,1)}) %reduce-scatter.4.cloned.1.call-update) | async-done | bytes 2097168
  633.2 8.1 %all-to-all-start.1 = ((bf16[8,32,4096]{2,0,1:T(8,128)(2,1)}), bf16[8,32,4096]{2,0,1:T(8,128)(2,1)}, u32[]{:S(2)}, u32[]{:S(2)}) async-start(bf16[8,32,4096]{2,0,1:T(8,128)(2,1)} %bitcast.76), calls=%async_computation.1 | async-start | bytes 4194304 | tf_op jit(solution)/shard_map/all_to_all | solution.py:160
  642.4 27.1 %all-to-all-done.1 = bf16[8,32,4096]{2,0,1:T(8,128)(2,1)} async-done(((bf16[8,32,4096]{2,0,1:T(8,128)(2,1)}), bf16[8,32,4096]{2,0,1:T(8,128)(2,1)}, u32[]{:S(2)}, u32[]{:S(2)}) %all-to-all-start.1) | async-done | bytes 2097184 | tf_op jit(solution)/shard_map/all_to_all | solution.py:160
  669.5 2.7 copy.120
  672.3 1.2 gather_fusion
  673.5 1.3 reshape.178
  674.8 2.7 reduce_sum.60
  677.5 0.6 reduce_sum.61
  678.2 1.4 multiply_reduce_fusion.1
  679.6 1.8 add_convert_fusion
  (71 shorter events, 2.1 us)
Async XLA Ops:
  6.5 3.1 copy-start
  6.5 61.5 %all-gather.3.cloned.1.call-start = ((), (), s32[]{:S(2)}) async-start(), calls=%async_computation.3 | async-start | bytes 8785920 | tf_op jit(solution)/shard_map/all_gather | solution.py:17
  10.9 118.5 %all-gather.5.cloned.1.call-start = ((), (), s32[]{:S(2)}) async-start(), calls=%async_computation.4 | async-start | bytes 8650752 | tf_op jit(solution)/shard_map/all_gather | solution.py:118
  11.7 365.1 %all-reduce.2.cloned.1.call-start = ((), (), s32[]{:S(2)}) async-start(), calls=%async_computation.5 | async-start | bytes 2097152 | tf_op jit(solution)/shard_map/psum | solution.py:128
  78.4 3.1 copy-start.5
  78.4 3.1 copy-start.7
  78.4 3.6 copy-start.9
  78.4 3.6 copy-start.13
  78.5 5.2 copy-start.6
  81.5 47.9 %copy-start.12 = (f32[1024]{0:T(1024)S(1)}, f32[1024]{0:T(1024)}, u32[]{:S(2)}) copy-start(f32[1024]{0:T(1024)} %param.27) | copy-start | bytes 12292
  92.3 43.3 %copy-start.10 = (s32[128,2]{0,1:T(2,128)S(1)}, s32[128,2]{0,1:T(2,128)}, u32[]{:S(2)}) copy-start(s32[128,2]{0,1:T(2,128)} %param.34) | copy-start | bytes 3076
  92.3 284.4 %copy-start.3 = (bf16[128,4096]{1,0:T(8,128)(2,1)S(1)}, bf16[128,4096]{1,0:T(8,128)(2,1)}, u32[]{:S(2)}) copy-start(bf16[128,4096]{1,0:T(8,128)(2,1)} %param.29) | copy-start | bytes 3145732
  135.3 244.5 %copy-start.8 = (f32[4096]{0:T(1024)S(1)}, f32[4096]{0:T(1024)}, u32[]{:S(2)}) copy-start(f32[4096]{0:T(1024)} %param.30) | copy-start | bytes 49156
  135.3 498.0 %reduce-scatter.4.cloned.1.call-start = ((), (), s32[]{:S(2)}) async-start(), calls=%async_computation.6 | async-start | bytes 10485760
  376.8 3.0 copy-start.4
  499.6 24.0 %slice-start = ((s8[7340032]{0:T(1024)(128)(4,1)}), s8[3145728]{0:T(1024)(128)(4,1)S(1)}, s32[]{:S(2)}) async-start(s8[7340032]{0:T(1024)(128)(4,1)} %bitcast.80), calls=%async_computation.7 | async-start | bytes 6291456
  511.0 12.7 %copy-start.2 = (bf16[32,32,4096]{2,1,0:T(8,128)(2,1)S(1)}, bf16[32,32,4096]{2,1,0:T(8,128)(2,1)}, u32[]{:S(2)}) copy-start(bf16[32,32,4096]{2,1,0:T(8,128)(2,1)} %copy.118) | copy-start | bytes 25165828
  511.0 12.7 %slice-start.1 = ((s8[7340032]{0:T(1024)(128)(4,1)}), s8[4194304]{0:T(1024)(128)(4,1)S(1)}, s32[]{:S(2)}) async-start(s8[7340032]{0:T(1024)(128)(4,1)} %bitcast.80), calls=%async_computation.8 | async-start | bytes 8388608
  511.0 21.9 %slice-start.2 = ((s8[7340032]{0:T(1024)(128)(4,1)}), s8[4194304]{0:T(1024)(128)(4,1)S(1)}, s32[]{:S(2)}) async-start(s8[7340032]{0:T(1024)(128)(4,1)} %bitcast.82), calls=%async_computation.9 | async-start | bytes 8388608
  523.7 9.2 %slice-start.3 = ((s8[7340032]{0:T(1024)(128)(4,1)}), s8[3145728]{0:T(1024)(128)(4,1)S(1)}, s32[]{:S(2)}) async-start(s8[7340032]{0:T(1024)(128)(4,1)} %bitcast.82), calls=%async_computation.10 | async-start | bytes 6291456
  555.5 86.8 %copy-start.11 = (f32[128,2]{0,1:T(2,128)S(1)}, f32[128,2]{0,1:T(2,128)}, u32[]{:S(2)}) copy-start(f32[128,2]{0,1:T(2,128)} %param.35) | copy-start | bytes 3076
  633.2 36.3 %all-to-all-start.1 = ((bf16[8,32,4096]{2,0,1:T(8,128)(2,1)}), bf16[8,32,4096]{2,0,1:T(8,128)(2,1)}, u32[]{:S(2)}, u32[]{:S(2)}) async-start(bf16[8,32,4096]{2,0,1:T(8,128)(2,1)} %bitcast.76), calls=%async_computation.1 | async-start | bytes 4194304 | tf_op jit(solution)/shard_map/all_to_all | solution.py:160
  673.5 8.0 %copy-start.1 = (bf16[128,128]{1,0:T(8,128)(2,1)S(1)}, bf16[128,128]{1,0:T(8,128)(2,1)}, u32[]{:S(2)}) copy-start(bf16[128,128]{1,0:T(8,128)(2,1)} %param.21) | copy-start | bytes 98308
Sparse Core Ops, SparseCore 0:
  11.0 56.9 all-gather.2
  70.2 59.1 all-gather.4
  135.4 241.3 all-reduce.1
  555.6 77.6 reduce-scatter.3
where the time goes:
time: 696 us; the launch traced here: 688 us
  waiting for transfers between devices  439 us (63%)
  blocking collectives  114 us (16%)
  local copies, waits for them, and re-layouts  52.4 us (8%)
  matrix products  43.4 us (6%)
  other arithmetic  17.9 us (3%)
  between operations  13.8 us (2%)
  starting transfers between devices  8.55 us (1%)
    psum x1, waiting for transfers between devices, local(): lax.psum(partial_value.astype(jnp.bfloat16), 'exp').astype(jnp.float32)  240 us
    all_to_all x1, blocking collectives, local(): lax.all_to_all(outgoing, 'ctx', split_axis=1, concat_axis=1, tiled=True)  105 us
    unnamed x5, waiting for transfers between devices  78.5 us
    all_gather x1, waiting for transfers between devices, entering(): gathered = lax.all_gather(packed.astype(jnp.bfloat16), axis)  55.4 us
    all_gather x1, waiting for transfers between devices, local(): lax.all_gather(out_proj, 'ctx', axis=1, tiled=True)  37.1 us
    all_to_all x1, waiting for transfers between devices, local(): lax.all_to_all(summed, 'ctx', split_axis=1, concat_axis=1, tiled=True)  27.1 us
  transfers between devices with their start and end apart: 5, of which 5 were waited for; matrix products, arithmetic and copies ran while one was open for 3% of the time, Pallas kernels for 0%

commit v1 on v0

--- a/solution.py
+++ b/solution.py
@@ -125,7 +125,9 @@
     first_row = lax.axis_index("exp") * tok_quarter
     own_ids = lax.dynamic_slice_in_dim(route_ids, first_row, tok_quarter, 0)
     own_gates = lax.dynamic_slice_in_dim(route_gates, first_row, tok_quarter, 0)
-    mixed_all = lax.psum(partial_value.astype(jnp.bfloat16), "exp").astype(jnp.float32)
+    mixed_all = jnp.sum(lax.all_gather(partial_value.astype(jnp.bfloat16), "exp"), axis=0).astype(
+        jnp.float32
+    )
     hidden_all = residual.astype(jnp.float32) + mixed_all
     moe_all = rms_rows(hidden_all, moe_gain)
 

time: 696 us -> 700 us (level)
    all_gather x0 -> x1, waiting for transfers between devices: none -> 244 us  [local(): lax.all_gather(partial_value.astype(jnp.bfloat16), 'exp')]
    psum x1 -> x0, waiting for transfers between devices: 240 us -> none  [local(): lax.psum(partial_value.astype(jnp.bfloat16), 'exp').astype(jnp.float32)]
where the time goes in v1:
time: 700 us; the launch traced here: 692 us
  waiting for transfers between devices  442 us (63%)
  blocking collectives  112 us (16%)
  local copies, waits for them, and re-layouts  52.4 us (7%)
  matrix products  43.3 us (6%)
  other arithmetic  19.7 us (3%)
  between operations  13.8 us (2%)
  starting transfers between devices  8.54 us (1%)
    all_gather x1, waiting for transfers between devices, local(): lax.all_gather(partial_value.astype(jnp.bfloat16), 'exp')  244 us
    all_to_all x1, blocking collectives, local(): lax.all_to_all(outgoing, 'ctx', split_axis=1, concat_axis=1, tiled=True)  104 us
    unnamed x5, waiting for transfers between devices  78 us
    all_gather x1, waiting for transfers between devices, entering(): gathered = lax.all_gather(packed.astype(jnp.bfloat16), axis)  55.4 us
    all_gather x1, waiting for transfers between devices, local(): lax.all_gather(out_proj, 'ctx', axis=1, tiled=True)  37.1 us
    all_to_all x1, waiting for transfers between devices, local(): lax.all_to_all(summed, 'ctx', split_axis=1, concat_axis=1, tiled=True)  27.1 us
  transfers between devices with their start and end apart: 5, of which 5 were waited for; matrix products, arithmetic and copies ran while one was open for 3% of the time, Pallas kernels for 0%

profile of v1, /device:TPU:1, one launch (start us, length us, event | category | flops | bytes accessed | tf_op | source)
XLA Modules:
  0.0 692.0 jit_solution(1594911708345375927)
XLA Ops:
  6.5 1.0 reduce_window_sum.33
  7.7 0.8 exponential_bitcast_fusion
  8.5 1.1 copy.109
  9.6 0.4 fusion.11
  10.2 0.7 copy.110
  11.0 0.7 all-gather.7.cloned.1.call-update
  11.8 0.9 fusion.42
  12.6 55.4 %all-gather.5.cloned.1.call-done = bf16[32,16,65,128]{3,1,2,0:T(8,128)(2,1)} async-done(((bf16[1,16,65,128]{3,1,2,0:T(8,128)(2,1)}), bf16[32,16,65,128]{3,1,2,0:T(8,128)(2,1)}) %all-gather.5.cloned.1.call-update) | async-done | bytes 8519696 | tf_op jit(solution)/shard_map/all_gather | solution.py:17
  68.1 2.5 broadcast_in_dim.28
  70.5 7.9 %while.12 = (s32[]{:T(128)}, f32[16]{0:T(128)S(1)}, f32[16,64,128]{0,2,1:T(8,128)}, s32[]{:T(128)}, bf16[32,16,65,128]{3,1,2,0:T(8,128)(2,1)}, /*index=5*/s32[]{:T(128)}, s32[]{:T(128)}, s32[]{:T(128)}) while((s32[]{:T(128)}, f32[16]{0:T(128)S(1)}, f32[16,64,128]{0,2,1:T(8,128)}, s32[]{:T(128)}, bf16[32,16,65,128]{3,1,2,0:T(8,128)(2,1)}, ...), condition=%wide.region_2.3_spmd, body=%wide.region_1.2_spmd.sunk | while | flops 395285 | bytes 3437051 | solution.py:24
  70.5 1.0 constant_dynamic-slice_fusion.4
  71.5 1.4 copy.132
  72.9 0.5 bitcast_convert_fusion.2
  73.5 5.0 slice_add_fusion.2
  78.5 3.1 copy.112
  81.6 0.5 fusion.10
  82.1 1.4 fusion.9
  83.7 0.2 multiply_reduce_fusion.2
  83.9 8.4 %psum.7 = f32[128]{0:T(128)S(1)} all-reduce(f32[128]{0:T(128)S(1)} %multiply_reduce_fusion.2), channel_id=1, replica_groups=mesh['ctx'=32,'exp'=4] {'exp'}, use_global_device_ids=true, to_apply=%region_4.5 | all-reduce | flops 128 | bytes 1024 | tf_op jit(solution)/shard_map/psum | solution.py:113
  92.3 37.1 %all-gather.7.cloned.1.call-done = bf16[1024,4096]{1,0:T(8,128)(2,1)} async-done(((bf16[1024,128]{1,0:T(8,128)(2,1)}), bf16[1024,4096]{1,0:T(8,128)(2,1)}) %all-gather.7.cloned.1.call-update) | async-done | bytes 8388624 | tf_op jit(solution)/shard_map/all_gather | solution.py:118
  129.4 5.8 convolution_convert_fusion.2
  135.2 0.3 reduce-scatter.4.cloned.1.call-start
  136.1 0.2 select_reduce_fusion
  136.3 244.3 %all-gather.9.cloned.1.call-done = bf16[512,4096]{1,0:T(8,128)(2,1)} async-done(((bf16[128,4096]{1,0:T(8,128)(2,1)}), bf16[512,4096]{1,0:T(8,128)(2,1)}) %all-gather.9.cloned.1.call-update) | async-done | bytes 4194320 | tf_op jit(solution)/shard_map/all_gather | solution.py:128
  380.6 3.1 reduce_sum.69
  383.7 1.7 convert_add_fusion
  385.4 0.4 multiply_convert_fusion.1
  385.8 3.4 broadcast_in_dim.30
  389.3 2.7 reshape.163
  392.0 1.4 convolution_convert_fusion.1
  393.4 2.3 copy.117
  395.7 4.3 broadcast_in_dim.31
  400.0 103.9 %all_to_all.10 = bf16[32,32,4096]{2,0,1:T(8,128)(2,1)} all-to-all(bf16[32,32,4096]{2,0,1:T(8,128)(2,1)} %bitcast.71), channel_id=1, replica_groups=mesh['ctx'=32,'exp'=4] {'ctx'}, dimensions={1} | all-to-all | bytes 16777216 | tf_op jit(solution)/shard_map/all_to_all | solution.py:143
  503.9 11.3 %copy.118 = bf16[32,32,4096]{2,1,0:T(8,128)(2,1)} copy(bf16[32,32,4096]{2,0,1:T(8,128)(2,1)} %all_to_all.10) | data formatting | bytes 16777216 | tf_op jit(solution)/shard_map/all_to_all | solution.py:143
  515.2 12.7 %fusion.2 = f32[1024,896]{1,0:T(8,128)S(1)} fusion(bf16[1024,4096]{1,0:T(8,128)(2,1)} %bitcast.73, bf16[1,4096,896]{2,1,0:T(8,128)(2,1)} %param.32), kind=kOutput, calls=%fused_computation.8 | convolution fusion | flops 7516192768 | bytes 19398656 | tf_op jit(solution)/shard_map/dot_general | solution.py:146
  527.9 9.2 %multiply_convert_fusion = bf16[1024,896]{1,0:T(8,128)(2,1)S(1)} fusion(f32[1024,896]{1,0:T(8,128)S(1)} %fusion.2, bf16[1024,4096]{1,0:T(8,128)(2,1)S(1)} %bitcast.74, bf16[1,4096,896]{2,1,0:T(8,128)(2,1)S(1)} %bitcast.83), kind=kOutput, calls=%fused_computation.14 | convolution fusion | flops 7521697792 | bytes 21233664 | tf_op jit(solution)/shard_map/dot_general | solution.py:145
  537.1 11.3 %convolution_convert_fusion = bf16[1024,4096]{1,0:T(8,128)(2,1)} fusion(bf16[1024,896]{1,0:T(8,128)(2,1)S(1)} %multiply_convert_fusion, bf16[1,896,4096]{2,1,0:T(8,128)(2,1)S(1)} %bitcast.85), kind=kOutput, calls=%fused_computation.6 | convolution fusion | flops 7520387072 | bytes 17563648 | tf_op jit(solution)/shard_map/dot_general | solution.py:150
  548.4 11.3 %copy.130 = bf16[4,8,32,4096]{3,1,2,0:T(8,128)(2,1)} copy(bf16[4,8,32,4096]{3,2,1,0:T(8,128)(2,1)} %bitcast.75) | data formatting | bytes 16777216
  559.7 77.2 %reduce-scatter.4.cloned.1.call-done = bf16[8,131072]{1,0:T(8,128)(2,1)} async-done(((bf16[32,131072]{1,0:T(8,128)(2,1)}), bf16[8,131072]{1,0:T(8,128)(2,1)}) %reduce-scatter.4.cloned.1.call-update) | async-done | bytes 2097168
  637.0 8.1 %all-to-all-start.1 = ((bf16[8,32,4096]{2,0,1:T(8,128)(2,1)}), bf16[8,32,4096]{2,0,1:T(8,128)(2,1)}, u32[]{:S(2)}, u32[]{:S(2)}) async-start(bf16[8,32,4096]{2,0,1:T(8,128)(2,1)} %bitcast.78), calls=%async_computation.1 | async-start | bytes 4194304 | tf_op jit(solution)/shard_map/all_to_all | solution.py:162
  646.2 27.1 %all-to-all-done.1 = bf16[8,32,4096]{2,0,1:T(8,128)(2,1)} async-done(((bf16[8,32,4096]{2,0,1:T(8,128)(2,1)}), bf16[8,32,4096]{2,0,1:T(8,128)(2,1)}, u32[]{:S(2)}, u32[]{:S(2)}) %all-to-all-start.1) | async-done | bytes 2097184 | tf_op jit(solution)/shard_map/all_to_all | solution.py:162
  673.3 2.7 copy.120
  676.0 1.2 gather_fusion
  677.2 1.3 reshape.179
  678.6 2.7 reduce_sum.73
  681.3 0.6 reduce_sum.74
  681.9 1.4 multiply_reduce_fusion.1
  683.4 1.8 add_convert_fusion
  (70 shorter events, 2.2 us)
Async XLA Ops:
  6.5 3.1 copy-start
  6.5 61.5 %all-gather.5.cloned.1.call-start = ((), (), s32[]{:S(2)}) async-start(), calls=%async_computation.3 | async-start | bytes 8785920 | tf_op jit(solution)/shard_map/all_gather | solution.py:17
  10.9 118.5 %all-gather.7.cloned.1.call-start = ((), (), s32[]{:S(2)}) async-start(), calls=%async_computation.4 | async-start | bytes 8650752 | tf_op jit(solution)/shard_map/all_gather | solution.py:118
  11.7 368.9 %all-gather.9.cloned.1.call-start = ((), (), s32[]{:S(2)}) async-start(), calls=%async_computation.5 | async-start | bytes 5242880 | tf_op jit(solution)/shard_map/all_gather | solution.py:128
  78.4 3.1 copy-start.4
  78.4 3.1 copy-start.6
  78.4 3.6 copy-start.8
  78.5 3.6 copy-start.12
  78.5 5.2 copy-start.5
  81.6 47.9 %copy-start.11 = (f32[1024]{0:T(1024)S(1)}, f32[1024]{0:T(1024)}, u32[]{:S(2)}) copy-start(f32[1024]{0:T(1024)} %param.27) | copy-start | bytes 12292
  92.3 43.2 %copy-start.9 = (s32[128,2]{0,1:T(2,128)S(1)}, s32[128,2]{0,1:T(2,128)}, u32[]{:S(2)}) copy-start(s32[128,2]{0,1:T(2,128)} %param.34) | copy-start | bytes 3076
  135.2 248.5 %copy-start.3 = (bf16[128,4096]{1,0:T(8,128)(2,1)S(1)}, bf16[128,4096]{1,0:T(8,128)(2,1)}, u32[]{:S(2)}) copy-start(bf16[128,4096]{1,0:T(8,128)(2,1)} %param.29) | copy-start | bytes 3145732
  135.2 501.8 %reduce-scatter.4.cloned.1.call-start = ((), (), s32[]{:S(2)}) async-start(), calls=%async_computation.6 | async-start | bytes 10485760
  380.6 4.8 copy-start.7
  503.9 24.0 %slice-start = ((s8[7340032]{0:T(1024)(128)(4,1)}), s8[3145728]{0:T(1024)(128)(4,1)S(1)}, s32[]{:S(2)}) async-start(s8[7340032]{0:T(1024)(128)(4,1)} %bitcast.82), calls=%async_computation.7 | async-start | bytes 6291456
  515.2 12.7 %copy-start.2 = (bf16[32,32,4096]{2,1,0:T(8,128)(2,1)S(1)}, bf16[32,32,4096]{2,1,0:T(8,128)(2,1)}, u32[]{:S(2)}) copy-start(bf16[32,32,4096]{2,1,0:T(8,128)(2,1)} %copy.118) | copy-start | bytes 25165828
  515.2 12.7 %slice-start.1 = ((s8[7340032]{0:T(1024)(128)(4,1)}), s8[4194304]{0:T(1024)(128)(4,1)S(1)}, s32[]{:S(2)}) async-start(s8[7340032]{0:T(1024)(128)(4,1)} %bitcast.82), calls=%async_computation.8 | async-start | bytes 8388608
  515.2 21.9 %slice-start.2 = ((s8[7340032]{0:T(1024)(128)(4,1)}), s8[4194304]{0:T(1024)(128)(4,1)S(1)}, s32[]{:S(2)}) async-start(s8[7340032]{0:T(1024)(128)(4,1)} %bitcast.84), calls=%async_computation.9 | async-start | bytes 8388608
  527.9 9.2 %slice-start.3 = ((s8[7340032]{0:T(1024)(128)(4,1)}), s8[3145728]{0:T(1024)(128)(4,1)S(1)}, s32[]{:S(2)}) async-start(s8[7340032]{0:T(1024)(128)(4,1)} %bitcast.84), calls=%async_computation.10 | async-start | bytes 6291456
  559.7 86.3 %copy-start.10 = (f32[128,2]{0,1:T(2,128)S(1)}, f32[128,2]{0,1:T(2,128)}, u32[]{:S(2)}) copy-start(f32[128,2]{0,1:T(2,128)} %param.35) | copy-start | bytes 3076
  637.0 36.3 %all-to-all-start.1 = ((bf16[8,32,4096]{2,0,1:T(8,128)(2,1)}), bf16[8,32,4096]{2,0,1:T(8,128)(2,1)}, u32[]{:S(2)}, u32[]{:S(2)}) async-start(bf16[8,32,4096]{2,0,1:T(8,128)(2,1)} %bitcast.78), calls=%async_computation.1 | async-start | bytes 4194304 | tf_op jit(solution)/shard_map/all_to_all | solution.py:162
  677.2 8.0 %copy-start.1 = (bf16[128,128]{1,0:T(8,128)(2,1)S(1)}, bf16[128,128]{1,0:T(8,128)(2,1)}, u32[]{:S(2)}) copy-start(bf16[128,128]{1,0:T(8,128)(2,1)} %param.21) | copy-start | bytes 98308
Sparse Core Ops, SparseCore 0:
  11.1 56.9 all-gather.4
  70.2 59.1 all-gather.6
  135.3 245.2 all-gather.8
  559.8 77.0 reduce-scatter.3
